TPU v7x, 32 devices: a whole 2x2x4 slice. The times are simulated.
32 devices in a mesh: depth: 32 (over z, y, x, core).
Axes of the slice: x: 2, y: 2, z: 4, core: 2. Of those that a mesh axis runs over, the one named last changes fastest.
Arguments:
- w_in: bfloat16 [64, 512, 1024], P('depth'), may hold values from -0.25 to 0.25
- w_out: bfloat16 [64, 1024, 512], P('depth'), may hold values from -0.0234375 to 0.0234375
- checkpoint: bfloat16 [32, 256, 512], P('depth'), may hold values from -6 to 6
- guess: float32 [32, 256, 512], P('depth'), may hold values from -6 to 6
- terminal: float32 [256, 512], replicated, may hold values from -6 to 6
Outputs:
- adjoint: float32 [64, 256, 512], P('depth')
- grad_in: bfloat16 [64, 512, 1024], P('depth')
- grad_out: bfloat16 [64, 1024, 512], P('depth')
All inputs are finite; a program needn't handle non-finite values.
Results may differ from a plain program's by a relative error of at most 0.017.
Values sent between devices are 32-bit elements; how exact they have to be, the bound alone decides.
No kernel may reach another device: no remote copies, remote signals or barrier semaphores. Data moves between devices by JAX's collectives and lax.ppermute only.
A program may use at most 64 MiB of HBM per device.

v0:
```python
import functools

import jax
import jax.numpy as jnp
from jax import lax
from jax.experimental import pallas as pl
from jax.experimental.pallas import tpu as pltpu
from jax.sharding import PartitionSpec as P


CHUNKS = 2
FULL = ((0, 0), (1, 0), (1, 1), (4, 0), (4, 1), (7, 0), (7, 1))
F32, BF16 = jnp.float32, jnp.bfloat16
VMEM = pl.BlockSpec(memory_space=pltpu.VMEM)
ANY = pl.BlockSpec(memory_space=pl.ANY)


def dot(a, b):
    return jnp.dot(a, b, preferred_element_type=F32)


def held(value):
    return pltpu.with_memory_space_constraint(value, pltpu.VMEM)


def in_hbm(value):
    return pltpu.with_memory_space_constraint(value, pltpu.HBM)


def core():
    return lax.rem(lax.axis_index("depth"), 2)


def on_core(which):
    return pl.when(core() == which)


def tangent(vector, out_t, slope):
    return (dot(vector.astype(BF16), out_t) * slope).astype(BF16)


def apply_slot(value, factor, slot, rows, in3, out3, slope3):
    return value + factor * dot(tangent(value, out3[slot], slope3[slot, rows, :]), in3[slot])


def pack_kernel(start_h, w_in_h, w_out_h, packed, start, w_in, w_out, sems):
    copies = [
        pltpu.make_async_copy(w_in_h.at[0], w_in, sems.at[0]),
        pltpu.make_async_copy(w_out_h.at[0], w_out, sems.at[1]),
        pltpu.make_async_copy(start_h.at[0], start, sems.at[2]),
    ]
    for copy in copies:
        copy.start()
    d, ff = w_in.shape
    copies[0].wait()

    @on_core(0)
    def _():
        for i in range(ff // d):
            packed[i * d : (i + 1) * d, :] = w_in[:, i * d : (i + 1) * d].astype(F32)

    copies[1].wait()
    copies[2].wait()

    @on_core(0)
    def _():
        packed[ff : 2 * ff, :] = w_out[...].astype(F32)
        packed[2 * ff :, :] = start[...].astype(F32)


def forward_kernel(
    token, w_in_h, w_out_h, start, w_in0, w_out0,
    in3, out3, slope3, state_t, act_t,
    w_in1, w_out1, upper_v, sems,
):
    copies = [
        pltpu.make_async_copy(w_in_h.at[1], w_in1, sems.at[0]),
        pltpu.make_async_copy(w_out_h.at[1], w_out1, sems.at[1]),
    ]
    for copy in copies:
        copy.start()
    h_zero = jnp.tanh(dot(start[...], w_in0[...]))
    slope3[1] = 1.0 - h_zero * h_zero
    act_zero = h_zero.astype(BF16)
    act_t[0] = act_zero.T
    upper_v[...] = (start[...].astype(F32) + dot(act_zero, w_out0[...])).astype(BF16)
    copies[0].wait()
    h_one = jnp.tanh(dot(upper_v[...], w_in1[...]))
    slope3[2] = 1.0 - h_one * h_one
    act_t[1] = h_one.astype(BF16).T
    in3[1] = w_in0[...].T
    out3[1] = w_out0[...].T
    in3[2] = w_in1[...].T
    state_t[0] = start[...].T
    state_t[1] = upper_v[...].T
    copies[1].wait()
    out3[2] = w_out1[...].T


def residual_kernel(token, moved, guess, in3, out3, slope3, resid):
    @on_core(0)
    def _():
        rows = slice(None)
        odd = apply_slot(moved[...], 1.0, 2, rows, in3, out3, slope3)
        resid[...] = apply_slot(odd, 1.0, 1, rows, in3, out3, slope3) - guess[...]


def adopt_kernel(token, packed, in_i, out_i, slope_i, in3, out3, slope3):
    @on_core(1)
    def _():
        ff, d = in3.shape[1:]
        state = packed[2 * ff :, :].astype(BF16)
        for i in range(ff // d):
            rows = slice(i * d, (i + 1) * d)
            part = packed[rows, :].astype(BF16)
            h = jnp.tanh(dot(state, part))
            slope3[0, :, rows] = 1.0 - h * h
            in3[0, rows, :] = part.T
        out3[0] = packed[ff : 2 * ff, :].astype(BF16).T


def value_kernel(low, size, token, moved, terminal, guess, resid_even, in3, out3, slope3, above, resid, value):
    rows = pl.ds(low, size)
    at_end = lax.axis_index("depth") == lax.axis_size("depth") - 1

    @on_core(0)
    def _():
        above[...] = moved[rows, :]
        resid[...] = jnp.zeros(resid.shape, F32)
        value[...] = jnp.zeros(value.shape, F32)

    @on_core(1)
    def _():
        above[...] = moved[rows, :]

        @pl.when(at_end)
        def _():
            above[...] = terminal[rows, :]

        odd = apply_slot(above[...], 1.0, 2, rows, in3, out3, slope3)
        own = apply_slot(odd, 1.0, 1, rows, in3, out3, slope3) - guess[rows, :]
        resid[...] = own
        value[...] = apply_slot(own, 2.0, 0, rows, in3, out3, slope3) + resid_even[rows, :]


def phi_kernel(low, size, steps, period, phases, distance, counts, token, in3, out3, slope3, *refs):
    groups, left = [], list(refs)
    for count in counts:
        groups.append(left[:count])
        left = left[count:]
    vectors, addends, extras = groups
    results = left
    chip = lax.axis_index("depth") // 2
    chips = lax.axis_size("depth") // 2
    here = jnp.logical_and(core() == 1, chip + distance < chips)
    rows = pl.ds(low, size)
    idle = True

    def finish(total):
        for addend in addends:
            total = total + addend[...]
        results[0][...] = total
        for extra in extras:
            results[1][...] = total + extra[...]

    for phase, vector in zip(phases, vectors):
        active = jnp.logical_and(here, lax.rem(chip, period) == phase)
        idle = jnp.logical_and(idle, jnp.logical_not(active))

        @pl.when(active)
        def _(vector=vector):
            value = vector[...]
            for slot, factor in steps:
                value = apply_slot(value, factor, slot, rows, in3, out3, slope3)
            finish(value)

    @pl.when(idle)
    def _():
        finish(jnp.zeros(results[0].shape, F32))


def final_kernel(low, size, token, resid, guess, above0, in3, out3, slope3, *refs):
    arrived, upper, low_2, last_odd, even, above = refs
    chip = lax.axis_index("depth") // 2
    at_end = chip == lax.axis_size("depth") // 2 - 1
    odd = lax.rem(chip, 2) == 1
    rows = pl.ds(low, size)

    @on_core(1)
    def _():
        @pl.when(jnp.logical_not(odd))
        def _():
            above[...] = arrived[...]

        @pl.when(jnp.logical_and(odd, jnp.logical_not(at_end)))
        def _():
            above[...] = upper[...] + low_2[...]

        @pl.when(jnp.logical_and(odd, at_end))
        def _():
            above[...] = jnp.zeros(above.shape, F32)

        value = above[...]
        last = apply_slot(value, 2.0, 1, rows, in3, out3, slope3) + resid[...]
        last_odd[...] = last
        even[...] = guess[rows, :] + last
        above[...] = above0[...] + value


def settle(low, size, sent_even, sent_odd, above0, guess, even, above):
    @on_core(0)
    def _():
        even[...] = guess[pl.ds(low, size), :] + sent_even[...]
        above[...] = above0[...] + sent_odd[...]


def part_kernel(low, size, token, in3, out3, slope3, guess, sent_even, sent_odd, above0, even_1, above_1, even, odd, above_b, odd_b, tan, above_v):
    rows = pl.ds(low, size)

    @on_core(1)
    def _():
        even[...] = even_1[...]
        above_v[...] = above_1[...]

    settle(low, size, sent_even, sent_odd, above0, guess, even, above_v)
    value = above_v[...]
    above_b[...] = value.astype(BF16)
    tan_one = tangent(value, out3[2], slope3[2, rows, :])
    tan[1] = tan_one
    value = value + dot(tan_one, in3[2])
    odd[...] = value
    odd_b[...] = value.astype(BF16)
    tan[0] = tangent(value, out3[1], slope3[1, rows, :])


def finish_kernel(lows, sizes, token, in3, out3, slope3, guess, sent_even, sent_odd, above0, even_1, above_1, state_t, act_t, *refs):
    chunks = len(lows)
    parts = [refs[5 * i : 5 * i + 5] for i in range(chunks - 1)]
    adjoint, grad_in, grad_out, even, odd, above, grad_in_v, grad_out_v, sems = refs[5 * (chunks - 1) :]
    low, size = lows[-1], sizes[-1]
    rows = pl.ds(low, size)
    copies = []

    def send(source, target):
        copy = pltpu.make_async_copy(source, target, sems.at[len(copies)])
        copy.start()
        copies.append(copy)

    for i in range(chunks - 1):
        send(parts[i][0], adjoint.at[0, pl.ds(lows[i], sizes[i]), :])
        send(parts[i][1], adjoint.at[1, pl.ds(lows[i], sizes[i]), :])

    @on_core(1)
    def _():
        even[...] = even_1[...]
        above[...] = above_1[...]

    settle(low, size, sent_even, sent_odd, above0, guess, even, above)
    send(even, adjoint.at[0, rows, :])

    def product(left, earlier, last):
        return dot(left, jnp.concatenate([*earlier, last], 0)).astype(BF16)

    value = above[...]
    grad_out_v[1] = product(act_t[1], [part[2][...] for part in parts], value.astype(BF16))
    send(grad_out_v.at[1], grad_out.at[1])
    tan_one = tangent(value, out3[2], slope3[2, rows, :])
    grad_in_v[1] = product(state_t[1], [part[4][1] for part in parts], tan_one)
    send(grad_in_v.at[1], grad_in.at[1])
    value = value + dot(tan_one, in3[2])
    odd[...] = value
    send(odd, adjoint.at[1, rows, :])
    grad_out_v[0] = product(act_t[0], [part[3][...] for part in parts], value.astype(BF16))
    send(grad_out_v.at[0], grad_out.at[0])
    tan_zero = tangent(value, out3[1], slope3[1, rows, :])
    tangents = jnp.concatenate([*[part[4][0] for part in parts], tan_zero], 0)
    pieces = 2
    piece = state_t.shape[1] // pieces
    for i in range(pieces):
        some = pl.ds(i * piece, piece)
        grad_in_v[0, some, :] = dot(state_t[0, some, :], tangents).astype(BF16)
        send(grad_in_v.at[0, some, :], grad_in.at[0, some, :])
    for copy in copies:
        copy.wait()


def local(w_in, w_out, checkpoint, guess, terminal):
    count = lax.axis_size("depth")
    rows, d = terminal.shape
    ff = w_in.shape[2]
    edges = [rows * i // CHUNKS // 16 * 16 for i in range(CHUNKS + 1)]
    lows, sizes = edges[:-1], [high - low for low, high in zip(edges, edges[1:])]
    token = []

    def run(kernel, shapes, operands, from_hbm=0, outs=None, mib=16, **options):
        specs = [VMEM] * len(token) + [ANY] * from_hbm + [VMEM] * (len(operands) - from_hbm)
        results = pl.pallas_call(
            kernel,
            out_shape=tuple(shapes),
            in_specs=specs,
            out_specs=outs or [VMEM] * len(shapes),
            compiler_params=pltpu.CompilerParams(vmem_limit_bytes=mib * 2**20),
            **options,
        )(*token, *operands)
        if outs:
            return results
        results = [held(result) for result in results]
        token[:] = [results[-1]]
        return results

    def permute(value, route):
        return held(lax.ppermute(value, "depth", route))

    hops = [0]

    def shift(value, period, phase, distance):
        target = {c: c - distance for c in range(distance, count // 2) if c % period == phase}
        hops[0] += 1
        if divmod(hops[0] - 1, CHUNKS) not in FULL:
            return permute(value, [(2 * c + 1, 2 * b + 1) for c, b in target.items()])
        route, used = [], set()
        for c in sorted(set(target) - set(target.values()), reverse=True):
            chain = [c]
            while chain[-1] in target:
                chain.append(target[chain[-1]])
            used |= set(chain)
            pairs = list(zip(chain, chain[1:]))
            route += [(2 * a + 1, 2 * b + 1) for a, b in pairs] + [(2 * b, 2 * a) for a, b in pairs]
            route += [(2 * chain[-1] + 1, 2 * chain[-1]), (2 * c, 2 * c + 1)]
        for c in range(count // 2):
            if c not in used:
                route += [(2 * c, 2 * c + 1), (2 * c + 1, 2 * c)]
        return permute(value, route)

    swap = [(i, i + 1 - 2 * (i % 2)) for i in range(count)]
    to_core_0 = to_core_1 = swap

    def vmem(*shape, kind=F32):
        return pltpu.VMEM(shape, kind)

    guess = guess.reshape(rows, d)
    packed, start, w_in0, w_out0 = run(
        pack_kernel,
        (vmem(2 * ff + rows, d), vmem(rows, d, kind=BF16), vmem(d, ff, kind=BF16), vmem(ff, d, kind=BF16)),
        (in_hbm(checkpoint), in_hbm(w_in), in_hbm(w_out)),
        from_hbm=3,
        scratch_shapes=[pltpu.SemaphoreType.DMA((3,))],
    )
    packed = permute(packed, to_core_1)
    moved = permute(guess, [(i, (i - 1) % count) for i in range(count)])
    guess, terminal = held(guess), held(terminal)
    layers = (vmem(3, ff, d, kind=BF16), vmem(3, d, ff, kind=BF16), vmem(3, rows, ff))
    *weights, state_t, act_t = run(
        forward_kernel,
        (*layers, vmem(2, d, rows, kind=BF16), vmem(2, ff, rows, kind=BF16)),
        (in_hbm(w_in), in_hbm(w_out), start, w_in0, w_out0),
        from_hbm=2,
        mib=24,
        scratch_shapes=[
            vmem(d, ff, kind=BF16),
            vmem(ff, d, kind=BF16),
            vmem(rows, d, kind=BF16),
            pltpu.SemaphoreType.DMA((2,)),
        ],
    )
    (resid_even,) = run(residual_kernel, (vmem(rows, d),), (moved, guess, *weights))
    resid_even = permute(resid_even, to_core_1)
    weights = run(adopt_kernel, layers, (packed, *weights), input_output_aliases={2: 0, 3: 1, 4: 2})

    def phi(i, vectors, steps, period, phases, distance=1, addends=(), extras=()):
        counts = (len(vectors), len(addends), len(extras))
        return run(
            functools.partial(phi_kernel, lows[i], sizes[i], steps, period, phases, distance, counts),
            (vmem(sizes[i], d),) * (2 if extras else 1),
            (*weights, *vectors, *addends, *extras),
        )

    parts = range(CHUNKS)
    fill = [None] * CHUNKS
    above0, resid, values, upper, rhs, hop, point = (list(fill) for _ in range(7))
    both, second, third = ((1, 2.0), (0, 2.0)), ((0, 4.0),), ((0, 8.0),)
    for i in parts:
        above0[i], resid[i], values[i] = run(
            functools.partial(value_kernel, lows[i], sizes[i]),
            (vmem(sizes[i], d),) * 3,
            (moved, terminal, guess, resid_even, *weights),
        )
        upper[i] = shift(values[i], 1, 0, 1)
    for i in parts:
        (rhs[i],) = phi(i, [upper[i]], both, 1, (0,))
        hop[i] = shift(rhs[i], 2, 1, 1)
    resid_2, level_3, deep, low, sent = (list(fill) for _ in range(5))
    for i in parts:
        (point[i],) = phi(i, [hop[i]], second, 2, (0,), 1, (rhs[i],))
        hop[i] = shift(point[i], 2, 0, 1)
    for i in parts:
        (value,) = phi(i, [hop[i]], second, 2, (1,))
        hop[i] = shift(value, 2, 1, 1)
    for i in parts:
        (resid_2[i],) = phi(i, [hop[i]], second, 2, (0,))
        hop[i] = shift(resid_2[i], 4, 2, 2)
    for i in parts:
        (level_3[i],) = phi(i, [hop[i]], third, 4, (0,), 2, (resid_2[i],))
        hop[i] = shift(level_3[i], 4, 0, 2)
    for i in parts:
        (deep[i],) = phi(i, [hop[i]], third, 4, (2,), 2, (level_3[i], point[i]))
        low[i] = shift(deep[i], 2, 0, 1)
    for i in parts:
        (values[i],) = phi(i, [low[i]], second, 2, (1,), 1, (deep[i], values[i]))
        sent[i] = shift(values[i], 2, 1, 1)
    arrived = [(sent[i], upper[i], low[i]) for i in parts]

    sent_even = [permute(value, to_core_0) for value in values]
    lasts = []
    for i, (low, size) in enumerate(zip(lows, sizes)):
        odd, even, above = run(
            functools.partial(final_kernel, low, size),
            (vmem(size, d), vmem(size, d), vmem(size, d)),
            (resid[i], guess, above0[i], *weights, *arrived[i]),
        )
        lasts.append((guess, sent_even[i], permute(odd, to_core_0), above0[i], even, above))
    parts = []
    for low, size, last in zip(lows[:-1], sizes, lasts):
        parts += run(
            functools.partial(part_kernel, low, size),
            (
                vmem(size, d),
                vmem(size, d),
                vmem(size, d, kind=BF16),
                vmem(size, d, kind=BF16),
                vmem(2, size, ff, kind=BF16),
            ),
            (*weights, *last),
            scratch_shapes=[vmem(size, d)],
        )
    return run(
        functools.partial(finish_kernel, lows, sizes),
        (
            jax.ShapeDtypeStruct((2, rows, d), F32),
            jax.ShapeDtypeStruct((2, d, ff), BF16),
            jax.ShapeDtypeStruct((2, ff, d), BF16),
        ),
        (*weights, *lasts[-1], state_t, act_t, *parts),
        outs=[ANY] * 3,
        mib=24,
        scratch_shapes=[
            vmem(sizes[-1], d),
            vmem(sizes[-1], d),
            vmem(sizes[-1], d),
            vmem(2, d, ff, kind=BF16),
            vmem(2, ff, d, kind=BF16),
            pltpu.SemaphoreType.DMA((2 * CHUNKS + 5,)),
        ],
    )


def solution(mesh):
    split = P("depth", None, None)

    return jax.shard_map(
        local,
        mesh=mesh,
        in_specs=(split, split, split, split, P()),
        out_specs=(split, split, split),
        check_vma=False,
    )
```

profile of v0, /device:TPU:1, one launch (start us, length us, event | category | flops | bytes accessed | tf_op | source)
XLA Modules:
  0.0 79.8 jit_solution(128107420267487664)
XLA Ops:
  0.6 1.7 %shard_map.76 = (f32[2304,512]{1,0:T(8,128)S(1)}, bf16[256,512]{1,0:T(8,128)(2,1)S(1)}, bf16[512,1024]{1,0:T(8,128)(2,1)S(1)}, bf16[1024,512]{1,0:T(8,128)(2,1)S(1)}) custom-call(bf16[1,256,512]{2,1,0:T(8,128)(2,1)} %start_h.1, bf16[2,512,1024]{2,1,0:T(8,128)(2,1)} %w_in_h.3, bf16[2,1024,512]{2,1,0:T(8,128)(2,1)} %w_out_h.3), custom_call_target="tpu_custom_call" | custom-call | tf_op jit(solution)/shard_map/pallas_call | solution.py:297
  2.9 2.8 %shard_map.77 = (bf16[3,1024,512]{2,1,0:T(8,128)(2,1)S(1)}, bf16[3,512,1024]{2,1,0:T(8,128)(2,1)S(1)}, f32[3,256,1024]{2,1,0:T(8,128)S(1)}, bf16[2,512,256]{2,1,0:T(8,128)(2,1)S(1)}, bf16[2,1024,256]{2,1,0:T(8,128)(2,1)S(1)}) custom-call(bf16[1024,512]{1,0:T(8,128)(2,1)S(1)} %get-tuple-element.32.token.w_out0, bf16[2,512,1024]{2,1,0:T(8,128)(2,1)} %w_in_h.3, ...), custom_call_target="tpu_custom_call" | custom-call | tf_op jit(solution)/shard_map/pallas_call | solution.py:297
  5.7 6.4 %collective-permute-done.moved = f32[256,512]{1,0:T(8,128)S(1)} collective-permute-done((f32[256,512]{1,0:T(8,128)S(1)}, f32[256,512]{1,0:T(8,128)S(1)}, u32[]{:S(2)}, u32[]{:S(2)}) %collective-permute-start) | collective-permute-done | bytes 524320 | tf_op jit(solution)/shard_map/ppermute | solution.py:312
  12.1 5.7 %collective-permute-start.2 = (f32[256,512]{1,0:T(8,128)S(1)}, f32[256,512]{1,0:T(8,128)S(1)}, u32[]{:S(2)}, u32[]{:S(2)}) collective-permute-start(f32[256,512]{1,0:T(8,128)S(1)} %shard_map.78.token), channel_id=1, source_target_pairs={{0,1},{1,0},{2,3},{3,2},{4,5},{5,4},{6,7},{7,6},{8,9},{9,8},{10,11... | collective-permute-start | bytes 1572872 | tf_op jit(solution)/shard_map/ppermute | solution.py:312
  17.8 0.7 shard_map.79
  18.5 0.8 %collective-permute-done.2.resid_even = f32[256,512]{1,0:T(8,128)S(1)} collective-permute-done((f32[256,512]{1,0:T(8,128)S(1)}, f32[256,512]{1,0:T(8,128)S(1)}, u32[]{:S(2)}, u32[]{:S(2)}) %collective-permute-start.2) | collective-permute-done | bytes 524320 | tf_op jit(solution)/shard_map/ppermute | solution.py:312
  19.3 1.3 %shard_map.80 = (f32[128,512]{1,0:T(8,128)S(1)}, f32[128,512]{1,0:T(8,128)S(1)}, f32[128,512]{1,0:T(8,128)S(1)}) custom-call(f32[3,256,1024]{2,1,0:T(8,128)S(1)} %get-tuple-element.40.token.slope3, f32[256,512]{1,0:T(8,128)S(1)} %collective-permute-done.moved, f32[256,512]{1,0:T(8,128)S(1)} %copy-done.1, f32[256,512]{1,0:T(8,128)S(1)} %bitcast.3, ...), custom_call_target="tpu_custom_call" | custom-call | tf_op jit(solution)/shard_map/pallas_call | solution.py:297
  20.7 1.3 %shard_map.81 = (f32[128,512]{1,0:T(8,128)S(1)}, f32[128,512]{1,0:T(8,128)S(1)}, f32[128,512]{1,0:T(8,128)S(1)}) custom-call(f32[128,512]{1,0:T(8,128)S(1)} %get-tuple-element.43.token.refs_2_, f32[256,512]{1,0:T(8,128)S(1)} %collective-permute-done.moved, f32[256,512]{1,0:T(8,128)S(1)} %copy-done.1, f32[256,512]{1,0:T(8,128)S(1)} %bitcast.4, ...), custom_call_target="tpu_custom_call" | custom-call | tf_op jit(solution)/shard_map/pallas_call | solution.py:297
  22.0 1.3 %collective-permute-start.4 = (f32[128,512]{1,0:T(8,128)S(1)}, f32[128,512]{1,0:T(8,128)S(1)}, u32[]{:S(2)}, u32[]{:S(2)}) collective-permute-start(f32[128,512]{1,0:T(8,128)S(1)} %get-tuple-element.44.token.refs_2_), channel_id=1, source_target_pairs={{3,1},{5,3},{7,5},{9,7},{11,9},{13,11},{15,13},{17,15},{19,17},{21... | collective-permute-start | bytes 786440 | tf_op jit(solution)/shard_map/ppermute | solution.py:312
  23.3 2.6 %collective-permute-done.3.refs_0_.refs_1_ = f32[128,512]{1,0:T(8,128)S(1)} collective-permute-done((f32[128,512]{1,0:T(8,128)S(1)}, f32[128,512]{1,0:T(8,128)S(1)}, u32[]{:S(2)}, u32[]{:S(2)}) %collective-permute-start.3) | collective-permute-done | bytes 262176 | tf_op jit(solution)/shard_map/ppermute | solution.py:312
  25.9 0.9 %shard_map.82.token.refs_1_ = f32[128,512]{1,0:T(8,128)S(1)} custom-call(f32[128,512]{1,0:T(8,128)S(1)} %get-tuple-element.44.token.refs_2_, bf16[3,1024,512]{2,1,0:T(8,128)(2,1)S(1)} %get-tuple-element.41.in3, bf16[3,512,1024]{2,1,0:T(8,128)(2,1)S(1)} %get-tuple-element.42.out3, f32[3,256,1024]{2,1,0:T(8,128)S(1)} %get-tuple-element.40.token.slope3, ...), custom_call_target="tpu_custom_call" | custom-call | tf_op jit(solution)/shard_map/pallas_call | solution.py:297
  26.8 2.5 %collective-permute-start.5 = (f32[128,512]{1,0:T(8,128)S(1)}, f32[128,512]{1,0:T(8,128)S(1)}, u32[]{:S(2)}, u32[]{:S(2)}) collective-permute-start(f32[128,512]{1,0:T(8,128)S(1)} %shard_map.82.token.refs_1_), channel_id=1, source_target_pairs={{31,29},{28,30},{29,28},{30,31},{27,25},{24,26},{25,24},{26,27},{2... | collective-permute-start | bytes 786440 | tf_op jit(solution)/shard_map/ppermute | solution.py:312
  29.3 0.9 %shard_map.83.token.refs_1_ = f32[128,512]{1,0:T(8,128)S(1)} custom-call(f32[128,512]{1,0:T(8,128)S(1)} %shard_map.82.token.refs_1_, bf16[3,1024,512]{2,1,0:T(8,128)(2,1)S(1)} %get-tuple-element.41.in3, bf16[3,512,1024]{2,1,0:T(8,128)(2,1)S(1)} %get-tuple-element.42.out3, f32[3,256,1024]{2,1,0:T(8,128)S(1)} %get-tuple-element.40.token.slope3, ...), custom_call_target="tpu_custom_call" | custom-call | tf_op jit(solution)/shard_map/pallas_call | solution.py:297
  30.2 1.6 %collective-permute-start.6 = (f32[128,512]{1,0:T(8,128)S(1)}, f32[128,512]{1,0:T(8,128)S(1)}, u32[]{:S(2)}, u32[]{:S(2)}) collective-permute-start(f32[128,512]{1,0:T(8,128)S(1)} %shard_map.83.token.refs_1_), channel_id=1, source_target_pairs={{31,29},{28,30},{29,28},{30,31},{27,25},{24,26},{25,24},{26,27},{2... | collective-permute-start | bytes 786440 | tf_op jit(solution)/shard_map/ppermute | solution.py:312
  32.5 0.7 collective-permute-start.7
  33.2 3.6 %collective-permute-done.6.refs_0_ = f32[128,512]{1,0:T(8,128)S(1)} collective-permute-done((f32[128,512]{1,0:T(8,128)S(1)}, f32[128,512]{1,0:T(8,128)S(1)}, u32[]{:S(2)}, u32[]{:S(2)}) %collective-permute-start.6) | collective-permute-done | bytes 262176 | tf_op jit(solution)/shard_map/ppermute | solution.py:312
  37.3 0.7 collective-permute-start.8
  38.1 1.3 %collective-permute-start.9 = (f32[128,512]{1,0:T(8,128)S(1)}, f32[128,512]{1,0:T(8,128)S(1)}, u32[]{:S(2)}, u32[]{:S(2)}) collective-permute-start(f32[128,512]{1,0:T(8,128)S(1)} %shard_map.86.token), channel_id=1, source_target_pairs={{3,1},{7,5},{11,9},{15,13},{19,17},{23,21},{27,25},{31,29}} | collective-permute-start | bytes 786440 | tf_op jit(solution)/shard_map/ppermute | solution.py:312
  39.4 1.3 %collective-permute-start.10 = (f32[128,512]{1,0:T(8,128)S(1)}, f32[128,512]{1,0:T(8,128)S(1)}, u32[]{:S(2)}, u32[]{:S(2)}) collective-permute-start(f32[128,512]{1,0:T(8,128)S(1)} %shard_map.87.token), channel_id=1, source_target_pairs={{3,1},{7,5},{11,9},{15,13},{19,17},{23,21},{27,25},{31,29}} | collective-permute-start | bytes 786440 | tf_op jit(solution)/shard_map/ppermute | solution.py:312
  40.7 6.0 %collective-permute-done.9.refs_0_ = f32[128,512]{1,0:T(8,128)S(1)} collective-permute-done((f32[128,512]{1,0:T(8,128)S(1)}, f32[128,512]{1,0:T(8,128)S(1)}, u32[]{:S(2)}, u32[]{:S(2)}) %collective-permute-start.9) | collective-permute-done | bytes 262176 | tf_op jit(solution)/shard_map/ppermute | solution.py:312
  47.3 2.7 %collective-permute-done.10.refs_0_ = f32[128,512]{1,0:T(8,128)S(1)} collective-permute-done((f32[128,512]{1,0:T(8,128)S(1)}, f32[128,512]{1,0:T(8,128)S(1)}, u32[]{:S(2)}, u32[]{:S(2)}) %collective-permute-start.10) | collective-permute-done | bytes 262176 | tf_op jit(solution)/shard_map/ppermute | solution.py:312
  50.5 1.9 %collective-permute-done.11.refs_0_ = f32[128,512]{1,0:T(8,128)S(1)} collective-permute-done((f32[128,512]{1,0:T(8,128)S(1)}, f32[128,512]{1,0:T(8,128)S(1)}, u32[]{:S(2)}, u32[]{:S(2)}) %collective-permute-start.11) | collective-permute-done | bytes 262176 | tf_op jit(solution)/shard_map/ppermute | solution.py:312
  53.0 0.7 collective-permute-start.13
  53.6 2.1 %collective-permute-done.12.refs_0_ = f32[128,512]{1,0:T(8,128)S(1)} collective-permute-done((f32[128,512]{1,0:T(8,128)S(1)}, f32[128,512]{1,0:T(8,128)S(1)}, u32[]{:S(2)}, u32[]{:S(2)}) %collective-permute-start.12) | collective-permute-done | bytes 262176 | tf_op jit(solution)/shard_map/ppermute | solution.py:312
  56.2 0.7 collective-permute-start.14
  57.9 0.7 collective-permute-start.16
  58.8 9.3 %collective-permute-start.21 = (f32[128,512]{1,0:T(8,128)S(1)}, f32[128,512]{1,0:T(8,128)S(1)}, u32[]{:S(2)}, u32[]{:S(2)}) collective-permute-start(f32[128,512]{1,0:T(8,128)S(1)} %shard_map.95.token), channel_id=1, source_target_pairs={{0,1},{1,0},{2,3},{3,2},{4,5},{5,4},{6,7},{7,6},{8,9},{9,8},{10,11... | collective-permute-start | bytes 786440 | tf_op jit(solution)/shard_map/ppermute | solution.py:312
  68.1 2.9 %collective-permute-done.17.refs_0_ = f32[128,512]{1,0:T(8,128)S(1)} collective-permute-done((f32[128,512]{1,0:T(8,128)S(1)}, f32[128,512]{1,0:T(8,128)S(1)}, u32[]{:S(2)}, u32[]{:S(2)}) %collective-permute-start.17) | collective-permute-done | bytes 262176 | tf_op jit(solution)/shard_map/ppermute | solution.py:312
  71.6 2.7 %collective-permute-done.18.refs_0_ = f32[128,512]{1,0:T(8,128)S(1)} collective-permute-done((f32[128,512]{1,0:T(8,128)S(1)}, f32[128,512]{1,0:T(8,128)S(1)}, u32[]{:S(2)}, u32[]{:S(2)}) %collective-permute-start.18) | collective-permute-done | bytes 262176 | tf_op jit(solution)/shard_map/ppermute | solution.py:312
  74.9 0.8 shard_map.98
  75.7 0.7 collective-permute-done.22.sent_odd
  76.4 3.2 %shard_map.99 = (f32[2,256,512]{2,1,0:T(8,128)}, bf16[2,512,1024]{2,1,0:T(8,128)(2,1)}, bf16[2,1024,512]{2,1,0:T(8,128)(2,1)}) custom-call(bf16[2,128,1024]{2,1,0:T(8,128)(2,1)S(1)} %get-tuple-element.53.token.refs_4_, bf16[3,1024,512]{2,1,0:T(8,128)(2,1)S(1)} %get-tuple-element.41.in3, bf16[3,512,1024]{2,1,0:T(8,128)(2,1)S(1)} %get-tuple-element.42.out3, ...), custom_call_target="tpu_custom_call" | custom-call | tf_op jit(solution)/shard_map/pallas_call | solution.py:297
  (42 shorter events, 6.2 us)
Async XLA Ops:
  0.6 1.9 %copy-start = (f32[1,256,512]{2,1,0:T(8,128)S(1)}, f32[1,256,512]{2,1,0:T(8,128)}, u32[]{:S(2)}) copy-start(f32[1,256,512]{2,1,0:T(8,128)} %param.8) | copy-start | bytes 1572868
  2.3 15.5 %collective-permute-start.1 = (f32[2304,512]{1,0:T(8,128)S(1)}, f32[2304,512]{1,0:T(8,128)S(1)}, u32[]{:S(2)}, u32[]{:S(2)}) collective-permute-start(f32[2304,512]{1,0:T(8,128)S(1)} %get-tuple-element.39), channel_id=1, source_target_pairs={{0,1},{1,0},{2,3},{3,2},{4,5},{5,4},{6,7},{7,6},{8,9},{9,8},{10,11... | collective-permute-start | bytes 14155784 | tf_op jit(solution)/shard_map/ppermute | solution.py:312
  2.6 9.5 %collective-permute-start = (f32[256,512]{1,0:T(8,128)S(1)}, f32[256,512]{1,0:T(8,128)S(1)}, u32[]{:S(2)}, u32[]{:S(2)}) collective-permute-start(f32[256,512]{1,0:T(8,128)S(1)} %bitcast.1), channel_id=1, source_target_pairs={{0,31},{1,0},{2,1},{3,2},{4,3},{5,4},{6,5},{7,6},{8,7},{9,8},{10,9... | collective-permute-start | bytes 1572872 | tf_op jit(solution)/shard_map/ppermute | solution.py:312
  12.1 7.2 %copy-start.1 = (f32[256,512]{1,0:T(8,128)S(1)}, f32[256,512]{1,0:T(8,128)}, u32[]{:S(2)}) copy-start(f32[256,512]{1,0:T(8,128)} %terminal.3) | copy-start | bytes 1572868
  12.1 7.2 %collective-permute-start.2 = (f32[256,512]{1,0:T(8,128)S(1)}, f32[256,512]{1,0:T(8,128)S(1)}, u32[]{:S(2)}, u32[]{:S(2)}) collective-permute-start(f32[256,512]{1,0:T(8,128)S(1)} %shard_map.78.token), channel_id=1, source_target_pairs={{0,1},{1,0},{2,3},{3,2},{4,5},{5,4},{6,7},{7,6},{8,9},{9,8},{10,11... | collective-permute-start | bytes 1572872 | tf_op jit(solution)/shard_map/ppermute | solution.py:312
  20.6 5.3 %collective-permute-start.3 = (f32[128,512]{1,0:T(8,128)S(1)}, f32[128,512]{1,0:T(8,128)S(1)}, u32[]{:S(2)}, u32[]{:S(2)}) collective-permute-start(f32[128,512]{1,0:T(8,128)S(1)} %get-tuple-element.43.token.refs_2_), channel_id=1, source_target_pairs={{31,29},{29,27},{27,25},{25,23},{23,21},{21,19},{19,17},{17,15},{1... | collective-permute-start | bytes 786440 | tf_op jit(solution)/shard_map/ppermute | solution.py:312
  22.0 7.3 %collective-permute-start.4 = (f32[128,512]{1,0:T(8,128)S(1)}, f32[128,512]{1,0:T(8,128)S(1)}, u32[]{:S(2)}, u32[]{:S(2)}) collective-permute-start(f32[128,512]{1,0:T(8,128)S(1)} %get-tuple-element.44.token.refs_2_), channel_id=1, source_target_pairs={{3,1},{5,3},{7,5},{9,7},{11,9},{13,11},{15,13},{17,15},{19,17},{21... | collective-permute-start | bytes 786440 | tf_op jit(solution)/shard_map/ppermute | solution.py:312
  26.8 5.2 %collective-permute-start.5 = (f32[128,512]{1,0:T(8,128)S(1)}, f32[128,512]{1,0:T(8,128)S(1)}, u32[]{:S(2)}, u32[]{:S(2)}) collective-permute-start(f32[128,512]{1,0:T(8,128)S(1)} %shard_map.82.token.refs_1_), channel_id=1, source_target_pairs={{31,29},{28,30},{29,28},{30,31},{27,25},{24,26},{25,24},{26,27},{2... | collective-permute-start | bytes 786440 | tf_op jit(solution)/shard_map/ppermute | solution.py:312
  30.2 6.6 %collective-permute-start.6 = (f32[128,512]{1,0:T(8,128)S(1)}, f32[128,512]{1,0:T(8,128)S(1)}, u32[]{:S(2)}, u32[]{:S(2)}) collective-permute-start(f32[128,512]{1,0:T(8,128)S(1)} %shard_map.83.token.refs_1_), channel_id=1, source_target_pairs={{31,29},{28,30},{29,28},{30,31},{27,25},{24,26},{25,24},{26,27},{2... | collective-permute-start | bytes 786440 | tf_op jit(solution)/shard_map/ppermute | solution.py:312
  32.5 5.5 %collective-permute-start.7 = (f32[128,512]{1,0:T(8,128)S(1)}, f32[128,512]{1,0:T(8,128)S(1)}, u32[]{:S(2)}, u32[]{:S(2)}) collective-permute-start(f32[128,512]{1,0:T(8,128)S(1)} %shard_map.84.token.refs_2_), channel_id=1, source_target_pairs={{5,3},{9,7},{13,11},{17,15},{21,19},{25,23},{29,27}} | collective-permute-start | bytes 786440 | tf_op jit(solution)/shard_map/ppermute | solution.py:312
  37.3 2.0 %collective-permute-start.8 = (f32[128,512]{1,0:T(8,128)S(1)}, f32[128,512]{1,0:T(8,128)S(1)}, u32[]{:S(2)}, u32[]{:S(2)}) collective-permute-start(f32[128,512]{1,0:T(8,128)S(1)} %shard_map.85.token.refs_2_), channel_id=1, source_target_pairs={{5,3},{9,7},{13,11},{17,15},{21,19},{25,23},{29,27}} | collective-permute-start | bytes 786440 | tf_op jit(solution)/shard_map/ppermute | solution.py:312
  38.1 8.6 %collective-permute-start.9 = (f32[128,512]{1,0:T(8,128)S(1)}, f32[128,512]{1,0:T(8,128)S(1)}, u32[]{:S(2)}, u32[]{:S(2)}) collective-permute-start(f32[128,512]{1,0:T(8,128)S(1)} %shard_map.86.token), channel_id=1, source_target_pairs={{3,1},{7,5},{11,9},{15,13},{19,17},{23,21},{27,25},{31,29}} | collective-permute-start | bytes 786440 | tf_op jit(solution)/shard_map/ppermute | solution.py:312
  39.4 10.5 %collective-permute-start.10 = (f32[128,512]{1,0:T(8,128)S(1)}, f32[128,512]{1,0:T(8,128)S(1)}, u32[]{:S(2)}, u32[]{:S(2)}) collective-permute-start(f32[128,512]{1,0:T(8,128)S(1)} %shard_map.87.token), channel_id=1, source_target_pairs={{3,1},{7,5},{11,9},{15,13},{19,17},{23,21},{27,25},{31,29}} | collective-permute-start | bytes 786440 | tf_op jit(solution)/shard_map/ppermute | solution.py:312
  47.2 5.3 %collective-permute-start.11 = (f32[128,512]{1,0:T(8,128)S(1)}, f32[128,512]{1,0:T(8,128)S(1)}, u32[]{:S(2)}, u32[]{:S(2)}) collective-permute-start(f32[128,512]{1,0:T(8,128)S(1)} %shard_map.88.token.refs_1_), channel_id=1, source_target_pairs={{29,25},{24,28},{25,24},{28,29},{21,17},{16,20},{17,16},{20,21},{1... | collective-permute-start | bytes 786440 | tf_op jit(solution)/shard_map/ppermute | solution.py:312
  50.5 5.3 %collective-permute-start.12 = (f32[128,512]{1,0:T(8,128)S(1)}, f32[128,512]{1,0:T(8,128)S(1)}, u32[]{:S(2)}, u32[]{:S(2)}) collective-permute-start(f32[128,512]{1,0:T(8,128)S(1)} %shard_map.89.token.refs_1_), channel_id=1, source_target_pairs={{29,25},{24,28},{25,24},{28,29},{21,17},{16,20},{17,16},{20,21},{1... | collective-permute-start | bytes 786440 | tf_op jit(solution)/shard_map/ppermute | solution.py:312
  53.0 4.0 %collective-permute-start.13 = (f32[128,512]{1,0:T(8,128)S(1)}, f32[128,512]{1,0:T(8,128)S(1)}, u32[]{:S(2)}, u32[]{:S(2)}) collective-permute-start(f32[128,512]{1,0:T(8,128)S(1)} %shard_map.90.token.refs_1_), channel_id=1, source_target_pairs={{9,5},{17,13},{25,21}} | collective-permute-start | bytes 786440 | tf_op jit(solution)/shard_map/ppermute | solution.py:312
  56.2 1.4 %collective-permute-start.14 = (f32[128,512]{1,0:T(8,128)S(1)}, f32[128,512]{1,0:T(8,128)S(1)}, u32[]{:S(2)}, u32[]{:S(2)}) collective-permute-start(f32[128,512]{1,0:T(8,128)S(1)} %shard_map.91.token.refs_1_), channel_id=1, source_target_pairs={{9,5},{17,13},{25,21}} | collective-permute-start | bytes 786440 | tf_op jit(solution)/shard_map/ppermute | solution.py:312
  57.0 1.6 %collective-permute-start.15 = (f32[128,512]{1,0:T(8,128)S(1)}, f32[128,512]{1,0:T(8,128)S(1)}, u32[]{:S(2)}, u32[]{:S(2)}) collective-permute-start(f32[128,512]{1,0:T(8,128)S(1)} %shard_map.92.token.refs_1_), channel_id=1, source_target_pairs={{5,3},{9,7},{13,11},{17,15},{21,19},{25,23},{29,27}} | collective-permute-start | bytes 786440 | tf_op jit(solution)/shard_map/ppermute | solution.py:312
  57.9 0.8 collective-permute-start.16
  58.7 12.4 %collective-permute-start.17 = (f32[128,512]{1,0:T(8,128)S(1)}, f32[128,512]{1,0:T(8,128)S(1)}, u32[]{:S(2)}, u32[]{:S(2)}) collective-permute-start(f32[128,512]{1,0:T(8,128)S(1)} %shard_map.94.token), channel_id=1, source_target_pairs={{31,29},{28,30},{29,28},{30,31},{27,25},{24,26},{25,24},{26,27},{2... | collective-permute-start | bytes 786440 | tf_op jit(solution)/shard_map/ppermute | solution.py:312
  58.8 15.5 %collective-permute-start.18 = (f32[128,512]{1,0:T(8,128)S(1)}, f32[128,512]{1,0:T(8,128)S(1)}, u32[]{:S(2)}, u32[]{:S(2)}) collective-permute-start(f32[128,512]{1,0:T(8,128)S(1)} %shard_map.95.token), channel_id=1, source_target_pairs={{31,29},{28,30},{29,28},{30,31},{27,25},{24,26},{25,24},{26,27},{2... | collective-permute-start | bytes 786440 | tf_op jit(solution)/shard_map/ppermute | solution.py:312
  58.8 16.9 %collective-permute-start.21 = (f32[128,512]{1,0:T(8,128)S(1)}, f32[128,512]{1,0:T(8,128)S(1)}, u32[]{:S(2)}, u32[]{:S(2)}) collective-permute-start(f32[128,512]{1,0:T(8,128)S(1)} %shard_map.95.token), channel_id=1, source_target_pairs={{0,1},{1,0},{2,3},{3,2},{4,5},{5,4},{6,7},{7,6},{8,9},{9,8},{10,11... | collective-permute-start | bytes 786440 | tf_op jit(solution)/shard_map/ppermute | solution.py:312
  68.1 6.8 %collective-permute-start.19 = (f32[128,512]{1,0:T(8,128)S(1)}, f32[128,512]{1,0:T(8,128)S(1)}, u32[]{:S(2)}, u32[]{:S(2)}) collective-permute-start(f32[128,512]{1,0:T(8,128)S(1)} %shard_map.94.token), channel_id=1, source_target_pairs={{0,1},{1,0},{2,3},{3,2},{4,5},{5,4},{6,7},{7,6},{8,9},{9,8},{10,11... | collective-permute-start | bytes 786440 | tf_op jit(solution)/shard_map/ppermute | solution.py:312
  71.6 3.4 %collective-permute-start.20 = (f32[128,512]{1,0:T(8,128)S(1)}, f32[128,512]{1,0:T(8,128)S(1)}, u32[]{:S(2)}, u32[]{:S(2)}) collective-permute-start(f32[128,512]{1,0:T(8,128)S(1)} %get-tuple-element.51), channel_id=1, source_target_pairs={{0,1},{1,0},{2,3},{3,2},{4,5},{5,4},{6,7},{7,6},{8,9},{9,8},{10,11... | collective-permute-start | bytes 786440 | tf_op jit(solution)/shard_map/ppermute | solution.py:312
  74.8 1.6 %collective-permute-start.22 = (f32[128,512]{1,0:T(8,128)S(1)}, f32[128,512]{1,0:T(8,128)S(1)}, u32[]{:S(2)}, u32[]{:S(2)}) collective-permute-start(f32[128,512]{1,0:T(8,128)S(1)} %get-tuple-element.54), channel_id=1, source_target_pairs={{0,1},{1,0},{2,3},{3,2},{4,5},{5,4},{6,7},{7,6},{8,9},{9,8},{10,11... | collective-permute-start | bytes 786440 | tf_op jit(solution)/shard_map/ppermute | solution.py:312
where the time goes:
time: 80.2 us; the launch traced here: 79.8 us
  waiting for transfers between devices  32.6 us (41%)
  starting transfers between devices  28.1 us (35%)
  Pallas kernels  17.9 us (22%)
  between operations  1.18 us (1%)
    ppermute x23, waiting for transfers between devices, permute(): return held(lax.ppermute(value, 'depth', route))  32.6 us
    ppermute x23, starting transfers between devices, permute(): return held(lax.ppermute(value, 'depth', route))  28.1 us
    pallas_call x24, Pallas kernels, run(): pl.pallas_call(kernel, out_shape=tuple(shapes), in_specs=specs, out_specs...  17.9 us
  transfers between devices with their start and end apart: 23, of which 12 were waited for; matrix products, arithmetic and copies ran while one was open for 0% of the time, Pallas kernels for 15%

commit v1 on v0

--- a/solution.py
+++ b/solution.py
@@ -70,8 +70,8 @@
 
 def forward_kernel(
     token, w_in_h, w_out_h, start, w_in0, w_out0,
-    in3, out3, slope3, state_t, act_t,
-    w_in1, w_out1, upper_v, sems,
+    in3, out3, slope3, upper, act,
+    w_in1, w_out1, sems,
 ):
     copies = [
         pltpu.make_async_copy(w_in_h.at[1], w_in1, sems.at[0]),
@@ -82,19 +82,24 @@
     h_zero = jnp.tanh(dot(start[...], w_in0[...]))
     slope3[1] = 1.0 - h_zero * h_zero
     act_zero = h_zero.astype(BF16)
-    act_t[0] = act_zero.T
-    upper_v[...] = (start[...].astype(F32) + dot(act_zero, w_out0[...])).astype(BF16)
+    act[0] = act_zero
+    upper[...] = (start[...].astype(F32) + dot(act_zero, w_out0[...])).astype(BF16)
     copies[0].wait()
-    h_one = jnp.tanh(dot(upper_v[...], w_in1[...]))
+    h_one = jnp.tanh(dot(upper[...], w_in1[...]))
     slope3[2] = 1.0 - h_one * h_one
-    act_t[1] = h_one.astype(BF16).T
+    act[1] = h_one.astype(BF16)
     in3[1] = w_in0[...].T
     out3[1] = w_out0[...].T
     in3[2] = w_in1[...].T
-    state_t[0] = start[...].T
-    state_t[1] = upper_v[...].T
     copies[1].wait()
     out3[2] = w_out1[...].T
+
+
+def turn_kernel(token, start, upper, act, state_t, act_t):
+    state_t[0] = start[...].T
+    state_t[1] = upper[...].T
+    act_t[0] = act[0].T
+    act_t[1] = act[1].T
 
 
 def residual_kernel(token, moved, guess, in3, out3, slope3, resid):
@@ -350,16 +355,15 @@
     moved = permute(guess, [(i, (i - 1) % count) for i in range(count)])
     guess, terminal = held(guess), held(terminal)
     layers = (vmem(3, ff, d, kind=BF16), vmem(3, d, ff, kind=BF16), vmem(3, rows, ff))
-    *weights, state_t, act_t = run(
+    *weights, upper_state, act = run(
         forward_kernel,
-        (*layers, vmem(2, d, rows, kind=BF16), vmem(2, ff, rows, kind=BF16)),
+        (*layers, vmem(rows, d, kind=BF16), vmem(2, rows, ff, kind=BF16)),
         (in_hbm(w_in), in_hbm(w_out), start, w_in0, w_out0),
         from_hbm=2,
         mib=24,
         scratch_shapes=[
             vmem(d, ff, kind=BF16),
             vmem(ff, d, kind=BF16),
-            vmem(rows, d, kind=BF16),
             pltpu.SemaphoreType.DMA((2,)),
         ],
     )
@@ -386,6 +390,11 @@
             (moved, terminal, guess, resid_even, *weights),
         )
         upper[i] = shift(values[i], 1, 0, 1)
+    state_t, act_t = run(
+        turn_kernel,
+        (vmem(2, d, rows, kind=BF16), vmem(2, ff, rows, kind=BF16)),
+        (start, upper_state, act),
+    )
     for i in parts:
         (rhs[i],) = phi(i, [upper[i]], both, 1, (0,))
         hop[i] = shift(rhs[i], 2, 1, 1)

time: 80.2 us -> 80.2 us (level)
    pallas_call x24 -> x25, Pallas kernels: 17.9 us -> 17.9 us  [run(): pl.pallas_call(kernel, out_shape=tuple(shapes), in_specs=specs, out_specs...]
where the time goes in v1:
time: 80.2 us; the launch traced here: 79.8 us
  waiting for transfers between devices  32.4 us (40%)
  starting transfers between devices  28.2 us (35%)
  Pallas kernels  17.9 us (22%)
  between operations  1.19 us (1%)
    ppermute x23, waiting for transfers between devices, permute(): return held(lax.ppermute(value, 'depth', route))  32.4 us
    ppermute x23, starting transfers between devices, permute(): return held(lax.ppermute(value, 'depth', route))  28.2 us
    pallas_call x25, Pallas kernels, run(): pl.pallas_call(kernel, out_shape=tuple(shapes), in_specs=specs, out_specs...  17.9 us
  transfers between devices with their start and end apart: 23, of which 12 were waited for; matrix products, arithmetic and copies ran while one was open for 0% of the time, Pallas kernels for 15%

profile of v1, /device:TPU:1, one launch (start us, length us, event | category | flops | bytes accessed | tf_op | source)
XLA Modules:
  0.0 79.8 jit_solution(3945303857586375484)
XLA Ops:
  0.6 1.7 %shard_map.76 = (f32[2304,512]{1,0:T(8,128)S(1)}, bf16[256,512]{1,0:T(8,128)(2,1)S(1)}, bf16[512,1024]{1,0:T(8,128)(2,1)S(1)}, bf16[1024,512]{1,0:T(8,128)(2,1)S(1)}) custom-call(bf16[1,256,512]{2,1,0:T(8,128)(2,1)} %start_h.1, bf16[2,512,1024]{2,1,0:T(8,128)(2,1)} %w_in_h.3, bf16[2,1024,512]{2,1,0:T(8,128)(2,1)} %w_out_h.3), custom_call_target="tpu_custom_call" | custom-call | tf_op jit(solution)/shard_map/pallas_call | solution.py:302
  2.9 2.5 %shard_map.77 = (bf16[3,1024,512]{2,1,0:T(8,128)(2,1)S(1)}, bf16[3,512,1024]{2,1,0:T(8,128)(2,1)S(1)}, f32[3,256,1024]{2,1,0:T(8,128)S(1)}, bf16[256,512]{1,0:T(8,128)(2,1)S(1)}, bf16[2,256,1024]{2,1,0:T(8,128)(2,1)S(1)}) custom-call(bf16[1024,512]{1,0:T(8,128)(2,1)S(1)} %get-tuple-element.34.token.w_out0, bf16[2,512,1024]{2,1,0:T(8,128)(2,1)} %w_in_h.3, ...), custom_call_target="tpu_custom_call" | custom-call | tf_op jit(solution)/shard_map/pallas_call | solution.py:302
  5.4 6.7 %collective-permute-done.moved = f32[256,512]{1,0:T(8,128)S(1)} collective-permute-done((f32[256,512]{1,0:T(8,128)S(1)}, f32[256,512]{1,0:T(8,128)S(1)}, u32[]{:S(2)}, u32[]{:S(2)}) %collective-permute-start) | collective-permute-done | bytes 524320 | tf_op jit(solution)/shard_map/ppermute | solution.py:317
  12.1 5.7 %collective-permute-start.2 = (f32[256,512]{1,0:T(8,128)S(1)}, f32[256,512]{1,0:T(8,128)S(1)}, u32[]{:S(2)}, u32[]{:S(2)}) collective-permute-start(f32[256,512]{1,0:T(8,128)S(1)} %shard_map.78.token), channel_id=1, source_target_pairs={{0,1},{1,0},{2,3},{3,2},{4,5},{5,4},{6,7},{7,6},{8,9},{9,8},{10,11... | collective-permute-start | bytes 1572872 | tf_op jit(solution)/shard_map/ppermute | solution.py:317
  17.8 0.7 shard_map.79
  18.5 0.8 %collective-permute-done.2.resid_even = f32[256,512]{1,0:T(8,128)S(1)} collective-permute-done((f32[256,512]{1,0:T(8,128)S(1)}, f32[256,512]{1,0:T(8,128)S(1)}, u32[]{:S(2)}, u32[]{:S(2)}) %collective-permute-start.2) | collective-permute-done | bytes 524320 | tf_op jit(solution)/shard_map/ppermute | solution.py:317
  19.3 1.3 %shard_map.80 = (f32[128,512]{1,0:T(8,128)S(1)}, f32[128,512]{1,0:T(8,128)S(1)}, f32[128,512]{1,0:T(8,128)S(1)}) custom-call(f32[3,256,1024]{2,1,0:T(8,128)S(1)} %get-tuple-element.42.token.slope3, f32[256,512]{1,0:T(8,128)S(1)} %collective-permute-done.moved, f32[256,512]{1,0:T(8,128)S(1)} %copy-done.1, f32[256,512]{1,0:T(8,128)S(1)} %bitcast.3, ...), custom_call_target="tpu_custom_call" | custom-call | tf_op jit(solution)/shard_map/pallas_call | solution.py:302
  20.7 1.3 %shard_map.81 = (f32[128,512]{1,0:T(8,128)S(1)}, f32[128,512]{1,0:T(8,128)S(1)}, f32[128,512]{1,0:T(8,128)S(1)}) custom-call(f32[128,512]{1,0:T(8,128)S(1)} %get-tuple-element.45.token.refs_2_, f32[256,512]{1,0:T(8,128)S(1)} %collective-permute-done.moved, f32[256,512]{1,0:T(8,128)S(1)} %copy-done.1, f32[256,512]{1,0:T(8,128)S(1)} %bitcast.4, ...), custom_call_target="tpu_custom_call" | custom-call | tf_op jit(solution)/shard_map/pallas_call | solution.py:302
  22.0 1.3 %collective-permute-start.4 = (f32[128,512]{1,0:T(8,128)S(1)}, f32[128,512]{1,0:T(8,128)S(1)}, u32[]{:S(2)}, u32[]{:S(2)}) collective-permute-start(f32[128,512]{1,0:T(8,128)S(1)} %get-tuple-element.46.token.refs_2_), channel_id=1, source_target_pairs={{3,1},{5,3},{7,5},{9,7},{11,9},{13,11},{15,13},{17,15},{19,17},{21... | collective-permute-start | bytes 786440 | tf_op jit(solution)/shard_map/ppermute | solution.py:317
  23.8 2.1 %collective-permute-done.3.refs_0_.refs_1_ = f32[128,512]{1,0:T(8,128)S(1)} collective-permute-done((f32[128,512]{1,0:T(8,128)S(1)}, f32[128,512]{1,0:T(8,128)S(1)}, u32[]{:S(2)}, u32[]{:S(2)}) %collective-permute-start.3) | collective-permute-done | bytes 262176 | tf_op jit(solution)/shard_map/ppermute | solution.py:317
  25.9 0.9 %shard_map.83.token.refs_1_ = f32[128,512]{1,0:T(8,128)S(1)} custom-call(bf16[2,1024,256]{2,1,0:T(8,128)(2,1)S(1)} %get-tuple-element.48.token.act_t, bf16[3,1024,512]{2,1,0:T(8,128)(2,1)S(1)} %get-tuple-element.43.in3, bf16[3,512,1024]{2,1,0:T(8,128)(2,1)S(1)} %get-tuple-element.44.out3, f32[3,256,1024]{2,1,0:T(8,128)S(1)} %get-tuple-element.42.token.slope3, ...), custom_call_target="tpu_custom_call" | custom-call | tf_op jit(solution)/shard_map/pallas_call | solution.py:302
  26.8 2.5 %collective-permute-start.5 = (f32[128,512]{1,0:T(8,128)S(1)}, f32[128,512]{1,0:T(8,128)S(1)}, u32[]{:S(2)}, u32[]{:S(2)}) collective-permute-start(f32[128,512]{1,0:T(8,128)S(1)} %shard_map.83.token.refs_1_), channel_id=1, source_target_pairs={{31,29},{28,30},{29,28},{30,31},{27,25},{24,26},{25,24},{26,27},{2... | collective-permute-start | bytes 786440 | tf_op jit(solution)/shard_map/ppermute | solution.py:317
  29.3 0.9 %shard_map.84.token.refs_1_ = f32[128,512]{1,0:T(8,128)S(1)} custom-call(f32[128,512]{1,0:T(8,128)S(1)} %shard_map.83.token.refs_1_, bf16[3,1024,512]{2,1,0:T(8,128)(2,1)S(1)} %get-tuple-element.43.in3, bf16[3,512,1024]{2,1,0:T(8,128)(2,1)S(1)} %get-tuple-element.44.out3, f32[3,256,1024]{2,1,0:T(8,128)S(1)} %get-tuple-element.42.token.slope3, ...), custom_call_target="tpu_custom_call" | custom-call | tf_op jit(solution)/shard_map/pallas_call | solution.py:302
  30.2 1.6 %collective-permute-start.6 = (f32[128,512]{1,0:T(8,128)S(1)}, f32[128,512]{1,0:T(8,128)S(1)}, u32[]{:S(2)}, u32[]{:S(2)}) collective-permute-start(f32[128,512]{1,0:T(8,128)S(1)} %shard_map.84.token.refs_1_), channel_id=1, source_target_pairs={{31,29},{28,30},{29,28},{30,31},{27,25},{24,26},{25,24},{26,27},{2... | collective-permute-start | bytes 786440 | tf_op jit(solution)/shard_map/ppermute | solution.py:317
  32.5 0.7 collective-permute-start.7
  33.2 3.6 %collective-permute-done.6.refs_0_ = f32[128,512]{1,0:T(8,128)S(1)} collective-permute-done((f32[128,512]{1,0:T(8,128)S(1)}, f32[128,512]{1,0:T(8,128)S(1)}, u32[]{:S(2)}, u32[]{:S(2)}) %collective-permute-start.6) | collective-permute-done | bytes 262176 | tf_op jit(solution)/shard_map/ppermute | solution.py:317
  37.3 0.7 collective-permute-start.8
  38.1 1.3 %collective-permute-start.9 = (f32[128,512]{1,0:T(8,128)S(1)}, f32[128,512]{1,0:T(8,128)S(1)}, u32[]{:S(2)}, u32[]{:S(2)}) collective-permute-start(f32[128,512]{1,0:T(8,128)S(1)} %shard_map.87.token), channel_id=1, source_target_pairs={{3,1},{7,5},{11,9},{15,13},{19,17},{23,21},{27,25},{31,29}} | collective-permute-start | bytes 786440 | tf_op jit(solution)/shard_map/ppermute | solution.py:317
  39.4 1.3 %collective-permute-start.10 = (f32[128,512]{1,0:T(8,128)S(1)}, f32[128,512]{1,0:T(8,128)S(1)}, u32[]{:S(2)}, u32[]{:S(2)}) collective-permute-start(f32[128,512]{1,0:T(8,128)S(1)} %shard_map.88.token), channel_id=1, source_target_pairs={{3,1},{7,5},{11,9},{15,13},{19,17},{23,21},{27,25},{31,29}} | collective-permute-start | bytes 786440 | tf_op jit(solution)/shard_map/ppermute | solution.py:317
  40.7 6.0 %collective-permute-done.9.refs_0_ = f32[128,512]{1,0:T(8,128)S(1)} collective-permute-done((f32[128,512]{1,0:T(8,128)S(1)}, f32[128,512]{1,0:T(8,128)S(1)}, u32[]{:S(2)}, u32[]{:S(2)}) %collective-permute-start.9) | collective-permute-done | bytes 262176 | tf_op jit(solution)/shard_map/ppermute | solution.py:317
  47.3 2.7 %collective-permute-done.10.refs_0_ = f32[128,512]{1,0:T(8,128)S(1)} collective-permute-done((f32[128,512]{1,0:T(8,128)S(1)}, f32[128,512]{1,0:T(8,128)S(1)}, u32[]{:S(2)}, u32[]{:S(2)}) %collective-permute-start.10) | collective-permute-done | bytes 262176 | tf_op jit(solution)/shard_map/ppermute | solution.py:317
  50.5 1.9 %collective-permute-done.11.refs_0_ = f32[128,512]{1,0:T(8,128)S(1)} collective-permute-done((f32[128,512]{1,0:T(8,128)S(1)}, f32[128,512]{1,0:T(8,128)S(1)}, u32[]{:S(2)}, u32[]{:S(2)}) %collective-permute-start.11) | collective-permute-done | bytes 262176 | tf_op jit(solution)/shard_map/ppermute | solution.py:317
  53.0 0.7 collective-permute-start.13
  53.6 2.1 %collective-permute-done.12.refs_0_ = f32[128,512]{1,0:T(8,128)S(1)} collective-permute-done((f32[128,512]{1,0:T(8,128)S(1)}, f32[128,512]{1,0:T(8,128)S(1)}, u32[]{:S(2)}, u32[]{:S(2)}) %collective-permute-start.12) | collective-permute-done | bytes 262176 | tf_op jit(solution)/shard_map/ppermute | solution.py:317
  57.0 0.9 %collective-permute-start.15 = (f32[128,512]{1,0:T(8,128)S(1)}, f32[128,512]{1,0:T(8,128)S(1)}, u32[]{:S(2)}, u32[]{:S(2)}) collective-permute-start(f32[128,512]{1,0:T(8,128)S(1)} %shard_map.93.token.refs_1_), channel_id=1, source_target_pairs={{5,3},{9,7},{13,11},{17,15},{21,19},{25,23},{29,27}} | collective-permute-start | bytes 786440 | tf_op jit(solution)/shard_map/ppermute | solution.py:317
  57.9 0.7 collective-permute-start.16
  58.8 9.3 %collective-permute-start.21 = (f32[128,512]{1,0:T(8,128)S(1)}, f32[128,512]{1,0:T(8,128)S(1)}, u32[]{:S(2)}, u32[]{:S(2)}) collective-permute-start(f32[128,512]{1,0:T(8,128)S(1)} %shard_map.96.token), channel_id=1, source_target_pairs={{0,1},{1,0},{2,3},{3,2},{4,5},{5,4},{6,7},{7,6},{8,9},{9,8},{10,11... | collective-permute-start | bytes 786440 | tf_op jit(solution)/shard_map/ppermute | solution.py:317
  68.1 2.9 %collective-permute-done.17.refs_0_ = f32[128,512]{1,0:T(8,128)S(1)} collective-permute-done((f32[128,512]{1,0:T(8,128)S(1)}, f32[128,512]{1,0:T(8,128)S(1)}, u32[]{:S(2)}, u32[]{:S(2)}) %collective-permute-start.17) | collective-permute-done | bytes 262176 | tf_op jit(solution)/shard_map/ppermute | solution.py:317
  71.6 2.7 %collective-permute-done.18.refs_0_ = f32[128,512]{1,0:T(8,128)S(1)} collective-permute-done((f32[128,512]{1,0:T(8,128)S(1)}, f32[128,512]{1,0:T(8,128)S(1)}, u32[]{:S(2)}, u32[]{:S(2)}) %collective-permute-start.18) | collective-permute-done | bytes 262176 | tf_op jit(solution)/shard_map/ppermute | solution.py:317
  74.9 0.8 shard_map.99
  75.7 0.7 collective-permute-done.22.sent_odd
  76.4 3.2 %shard_map.100 = (f32[2,256,512]{2,1,0:T(8,128)}, bf16[2,512,1024]{2,1,0:T(8,128)(2,1)}, bf16[2,1024,512]{2,1,0:T(8,128)(2,1)}) custom-call(bf16[2,128,1024]{2,1,0:T(8,128)(2,1)S(1)} %get-tuple-element.57.token.refs_4_, bf16[3,1024,512]{2,1,0:T(8,128)(2,1)S(1)} %get-tuple-element.43.in3, bf16[3,512,1024]{2,1,0:T(8,128)(2,1)S(1)} %get-tuple-element.44.out3, ...), custom_call_target="tpu_custom_call" | custom-call | tf_op jit(solution)/shard_map/pallas_call | solution.py:302
  (43 shorter events, 6.5 us)
Async XLA Ops:
  0.6 1.9 %copy-start = (f32[1,256,512]{2,1,0:T(8,128)S(1)}, f32[1,256,512]{2,1,0:T(8,128)}, u32[]{:S(2)}) copy-start(f32[1,256,512]{2,1,0:T(8,128)} %param.8) | copy-start | bytes 1572868
  2.3 15.5 %collective-permute-start.1 = (f32[2304,512]{1,0:T(8,128)S(1)}, f32[2304,512]{1,0:T(8,128)S(1)}, u32[]{:S(2)}, u32[]{:S(2)}) collective-permute-start(f32[2304,512]{1,0:T(8,128)S(1)} %get-tuple-element.41), channel_id=1, source_target_pairs={{0,1},{1,0},{2,3},{3,2},{4,5},{5,4},{6,7},{7,6},{8,9},{9,8},{10,11... | collective-permute-start | bytes 14155784 | tf_op jit(solution)/shard_map/ppermute | solution.py:317
  2.6 9.5 %collective-permute-start = (f32[256,512]{1,0:T(8,128)S(1)}, f32[256,512]{1,0:T(8,128)S(1)}, u32[]{:S(2)}, u32[]{:S(2)}) collective-permute-start(f32[256,512]{1,0:T(8,128)S(1)} %bitcast.1), channel_id=1, source_target_pairs={{0,31},{1,0},{2,1},{3,2},{4,3},{5,4},{6,5},{7,6},{8,7},{9,8},{10,9... | collective-permute-start | bytes 1572872 | tf_op jit(solution)/shard_map/ppermute | solution.py:317
  12.1 7.2 %copy-start.1 = (f32[256,512]{1,0:T(8,128)S(1)}, f32[256,512]{1,0:T(8,128)}, u32[]{:S(2)}) copy-start(f32[256,512]{1,0:T(8,128)} %terminal.3) | copy-start | bytes 1572868
  12.1 7.2 %collective-permute-start.2 = (f32[256,512]{1,0:T(8,128)S(1)}, f32[256,512]{1,0:T(8,128)S(1)}, u32[]{:S(2)}, u32[]{:S(2)}) collective-permute-start(f32[256,512]{1,0:T(8,128)S(1)} %shard_map.78.token), channel_id=1, source_target_pairs={{0,1},{1,0},{2,3},{3,2},{4,5},{5,4},{6,7},{7,6},{8,9},{9,8},{10,11... | collective-permute-start | bytes 1572872 | tf_op jit(solution)/shard_map/ppermute | solution.py:317
  20.6 5.3 %collective-permute-start.3 = (f32[128,512]{1,0:T(8,128)S(1)}, f32[128,512]{1,0:T(8,128)S(1)}, u32[]{:S(2)}, u32[]{:S(2)}) collective-permute-start(f32[128,512]{1,0:T(8,128)S(1)} %get-tuple-element.45.token.refs_2_), channel_id=1, source_target_pairs={{31,29},{29,27},{27,25},{25,23},{23,21},{21,19},{19,17},{17,15},{1... | collective-permute-start | bytes 786440 | tf_op jit(solution)/shard_map/ppermute | solution.py:317
  22.0 7.3 %collective-permute-start.4 = (f32[128,512]{1,0:T(8,128)S(1)}, f32[128,512]{1,0:T(8,128)S(1)}, u32[]{:S(2)}, u32[]{:S(2)}) collective-permute-start(f32[128,512]{1,0:T(8,128)S(1)} %get-tuple-element.46.token.refs_2_), channel_id=1, source_target_pairs={{3,1},{5,3},{7,5},{9,7},{11,9},{13,11},{15,13},{17,15},{19,17},{21... | collective-permute-start | bytes 786440 | tf_op jit(solution)/shard_map/ppermute | solution.py:317
  26.8 5.2 %collective-permute-start.5 = (f32[128,512]{1,0:T(8,128)S(1)}, f32[128,512]{1,0:T(8,128)S(1)}, u32[]{:S(2)}, u32[]{:S(2)}) collective-permute-start(f32[128,512]{1,0:T(8,128)S(1)} %shard_map.83.token.refs_1_), channel_id=1, source_target_pairs={{31,29},{28,30},{29,28},{30,31},{27,25},{24,26},{25,24},{26,27},{2... | collective-permute-start | bytes 786440 | tf_op jit(solution)/shard_map/ppermute | solution.py:317
  30.2 6.6 %collective-permute-start.6 = (f32[128,512]{1,0:T(8,128)S(1)}, f32[128,512]{1,0:T(8,128)S(1)}, u32[]{:S(2)}, u32[]{:S(2)}) collective-permute-start(f32[128,512]{1,0:T(8,128)S(1)} %shard_map.84.token.refs_1_), channel_id=1, source_target_pairs={{31,29},{28,30},{29,28},{30,31},{27,25},{24,26},{25,24},{26,27},{2... | collective-permute-start | bytes 786440 | tf_op jit(solution)/shard_map/ppermute | solution.py:317
  32.5 5.5 %collective-permute-start.7 = (f32[128,512]{1,0:T(8,128)S(1)}, f32[128,512]{1,0:T(8,128)S(1)}, u32[]{:S(2)}, u32[]{:S(2)}) collective-permute-start(f32[128,512]{1,0:T(8,128)S(1)} %shard_map.85.token.refs_2_), channel_id=1, source_target_pairs={{5,3},{9,7},{13,11},{17,15},{21,19},{25,23},{29,27}} | collective-permute-start | bytes 786440 | tf_op jit(solution)/shard_map/ppermute | solution.py:317
  37.3 2.0 %collective-permute-start.8 = (f32[128,512]{1,0:T(8,128)S(1)}, f32[128,512]{1,0:T(8,128)S(1)}, u32[]{:S(2)}, u32[]{:S(2)}) collective-permute-start(f32[128,512]{1,0:T(8,128)S(1)} %shard_map.86.token.refs_2_), channel_id=1, source_target_pairs={{5,3},{9,7},{13,11},{17,15},{21,19},{25,23},{29,27}} | collective-permute-start | bytes 786440 | tf_op jit(solution)/shard_map/ppermute | solution.py:317
  38.1 8.6 %collective-permute-start.9 = (f32[128,512]{1,0:T(8,128)S(1)}, f32[128,512]{1,0:T(8,128)S(1)}, u32[]{:S(2)}, u32[]{:S(2)}) collective-permute-start(f32[128,512]{1,0:T(8,128)S(1)} %shard_map.87.token), channel_id=1, source_target_pairs={{3,1},{7,5},{11,9},{15,13},{19,17},{23,21},{27,25},{31,29}} | collective-permute-start | bytes 786440 | tf_op jit(solution)/shard_map/ppermute | solution.py:317
  39.4 10.5 %collective-permute-start.10 = (f32[128,512]{1,0:T(8,128)S(1)}, f32[128,512]{1,0:T(8,128)S(1)}, u32[]{:S(2)}, u32[]{:S(2)}) collective-permute-start(f32[128,512]{1,0:T(8,128)S(1)} %shard_map.88.token), channel_id=1, source_target_pairs={{3,1},{7,5},{11,9},{15,13},{19,17},{23,21},{27,25},{31,29}} | collective-permute-start | bytes 786440 | tf_op jit(solution)/shard_map/ppermute | solution.py:317
  47.2 5.3 %collective-permute-start.11 = (f32[128,512]{1,0:T(8,128)S(1)}, f32[128,512]{1,0:T(8,128)S(1)}, u32[]{:S(2)}, u32[]{:S(2)}) collective-permute-start(f32[128,512]{1,0:T(8,128)S(1)} %shard_map.89.token.refs_1_), channel_id=1, source_target_pairs={{29,25},{24,28},{25,24},{28,29},{21,17},{16,20},{17,16},{20,21},{1... | collective-permute-start | bytes 786440 | tf_op jit(solution)/shard_map/ppermute | solution.py:317
  50.5 5.3 %collective-permute-start.12 = (f32[128,512]{1,0:T(8,128)S(1)}, f32[128,512]{1,0:T(8,128)S(1)}, u32[]{:S(2)}, u32[]{:S(2)}) collective-permute-start(f32[128,512]{1,0:T(8,128)S(1)} %shard_map.90.token.refs_1_), channel_id=1, source_target_pairs={{29,25},{24,28},{25,24},{28,29},{21,17},{16,20},{17,16},{20,21},{1... | collective-permute-start | bytes 786440 | tf_op jit(solution)/shard_map/ppermute | solution.py:317
  53.0 4.0 %collective-permute-start.13 = (f32[128,512]{1,0:T(8,128)S(1)}, f32[128,512]{1,0:T(8,128)S(1)}, u32[]{:S(2)}, u32[]{:S(2)}) collective-permute-start(f32[128,512]{1,0:T(8,128)S(1)} %shard_map.91.token.refs_1_), channel_id=1, source_target_pairs={{9,5},{17,13},{25,21}} | collective-permute-start | bytes 786440 | tf_op jit(solution)/shard_map/ppermute | solution.py:317
  56.2 1.6 %collective-permute-start.14 = (f32[128,512]{1,0:T(8,128)S(1)}, f32[128,512]{1,0:T(8,128)S(1)}, u32[]{:S(2)}, u32[]{:S(2)}) collective-permute-start(f32[128,512]{1,0:T(8,128)S(1)} %shard_map.92.token.refs_1_), channel_id=1, source_target_pairs={{9,5},{17,13},{25,21}} | collective-permute-start | bytes 786440 | tf_op jit(solution)/shard_map/ppermute | solution.py:317
  57.0 1.6 %collective-permute-start.15 = (f32[128,512]{1,0:T(8,128)S(1)}, f32[128,512]{1,0:T(8,128)S(1)}, u32[]{:S(2)}, u32[]{:S(2)}) collective-permute-start(f32[128,512]{1,0:T(8,128)S(1)} %shard_map.93.token.refs_1_), channel_id=1, source_target_pairs={{5,3},{9,7},{13,11},{17,15},{21,19},{25,23},{29,27}} | collective-permute-start | bytes 786440 | tf_op jit(solution)/shard_map/ppermute | solution.py:317
  57.9 0.8 collective-permute-start.16
  58.7 12.4 %collective-permute-start.17 = (f32[128,512]{1,0:T(8,128)S(1)}, f32[128,512]{1,0:T(8,128)S(1)}, u32[]{:S(2)}, u32[]{:S(2)}) collective-permute-start(f32[128,512]{1,0:T(8,128)S(1)} %shard_map.95.token), channel_id=1, source_target_pairs={{31,29},{28,30},{29,28},{30,31},{27,25},{24,26},{25,24},{26,27},{2... | collective-permute-start | bytes 786440 | tf_op jit(solution)/shard_map/ppermute | solution.py:317
  58.8 15.5 %collective-permute-start.18 = (f32[128,512]{1,0:T(8,128)S(1)}, f32[128,512]{1,0:T(8,128)S(1)}, u32[]{:S(2)}, u32[]{:S(2)}) collective-permute-start(f32[128,512]{1,0:T(8,128)S(1)} %shard_map.96.token), channel_id=1, source_target_pairs={{31,29},{28,30},{29,28},{30,31},{27,25},{24,26},{25,24},{26,27},{2... | collective-permute-start | bytes 786440 | tf_op jit(solution)/shard_map/ppermute | solution.py:317
  58.8 16.9 %collective-permute-start.21 = (f32[128,512]{1,0:T(8,128)S(1)}, f32[128,512]{1,0:T(8,128)S(1)}, u32[]{:S(2)}, u32[]{:S(2)}) collective-permute-start(f32[128,512]{1,0:T(8,128)S(1)} %shard_map.96.token), channel_id=1, source_target_pairs={{0,1},{1,0},{2,3},{3,2},{4,5},{5,4},{6,7},{7,6},{8,9},{9,8},{10,11... | collective-permute-start | bytes 786440 | tf_op jit(solution)/shard_map/ppermute | solution.py:317
  68.1 6.8 %collective-permute-start.19 = (f32[128,512]{1,0:T(8,128)S(1)}, f32[128,512]{1,0:T(8,128)S(1)}, u32[]{:S(2)}, u32[]{:S(2)}) collective-permute-start(f32[128,512]{1,0:T(8,128)S(1)} %shard_map.95.token), channel_id=1, source_target_pairs={{0,1},{1,0},{2,3},{3,2},{4,5},{5,4},{6,7},{7,6},{8,9},{9,8},{10,11... | collective-permute-start | bytes 786440 | tf_op jit(solution)/shard_map/ppermute | solution.py:317
  71.6 3.4 %collective-permute-start.20 = (f32[128,512]{1,0:T(8,128)S(1)}, f32[128,512]{1,0:T(8,128)S(1)}, u32[]{:S(2)}, u32[]{:S(2)}) collective-permute-start(f32[128,512]{1,0:T(8,128)S(1)} %get-tuple-element.55), channel_id=1, source_target_pairs={{0,1},{1,0},{2,3},{3,2},{4,5},{5,4},{6,7},{7,6},{8,9},{9,8},{10,11... | collective-permute-start | bytes 786440 | tf_op jit(solution)/shard_map/ppermute | solution.py:317
  74.8 1.6 %collective-permute-start.22 = (f32[128,512]{1,0:T(8,128)S(1)}, f32[128,512]{1,0:T(8,128)S(1)}, u32[]{:S(2)}, u32[]{:S(2)}) collective-permute-start(f32[128,512]{1,0:T(8,128)S(1)} %get-tuple-element.58), channel_id=1, source_target_pairs={{0,1},{1,0},{2,3},{3,2},{4,5},{5,4},{6,7},{7,6},{8,9},{9,8},{10,11... | collective-permute-start | bytes 786440 | tf_op jit(solution)/shard_map/ppermute | solution.py:317
